TPU v7x, 32 devices: a whole 2x2x4 slice. The times are simulated.
32 devices in a mesh: vel: 16 (over z, y, x), space: 2 (over core).
Axes of the slice: x: 2, y: 2, z: 4, core: 2. Of those that a mesh axis runs over, the one named last changes fastest.
Arguments:
- distribution: float32 [16384, 16, 128], P('vel', 'space'), may hold values from 0 to 11, as said below
- rate_class: int32 [16, 128], P('space'), may hold values from 0 to 7
- boundary_obstacle_indicator: int32 [16, 128], P('space'), may hold values 0 or 1
Outputs:
- field_out: float32 [16384, 16, 128], P('vel', 'space')
- latest_conserved_fields: float32 [5, 16, 128], P(None, 'space')
Inputs may be any that keep to these rules, and one draw needn't show every extreme that they name: `distribution`: every entry positive.
All inputs are finite; a program needn't handle non-finite values. No bound on the sum of `boundary_obstacle_indicator` on one device may be relied on, other than what follows from the above.
Results may differ from a plain program's by a relative error of at most 0.0003.
Values sent between devices are 32-bit elements; how exact they have to be, the bound alone decides.
A program may use at most 64 MiB of HBM per device.

v0:
```python
import jax
import jax.numpy as jnp
from jax import lax
from jax.sharding import PartitionSpec as P

VX = 32
VY = 32
VZ = 16
ITERS = 2
SWEEPS = 4
speed_edge = 5.0
marching_step_length = 0.1
momentum_thermal_ratio = 2.0 / 3.0
shear_power_law_index = 0.81
diffusivity = 1.0


def with_halo(value, sides, width):
    for axis, dim in sides:
        size, length = (lax.axis_size(axis), value.shape[dim])
        up = [(i, (i + 1) % size) for i in range(size)]
        down = [(j, i) for i, j in up]
        last = lax.slice_in_dim(value, length - width, length, axis=dim)
        leading = lax.slice_in_dim(value, 0, width, axis=dim)
        before = lax.ppermute(last, axis, up)
        after = lax.ppermute(leading, axis, down)
        value = jnp.concatenate([before, value, after], axis=dim)
    return value


def velocity_table(index):
    index_x = index % VX
    index_y = index // VX % VY
    index_z = index // (VX * VY)
    discrete_abscissa_xaxis = -speed_edge + (index_x.astype(jnp.float32) + 0.5) * (
        2.0 * speed_edge / VX
    )
    discrete_abscissa_yaxis = -speed_edge + (index_y.astype(jnp.float32) + 0.5) * (
        2.0 * speed_edge / VY
    )
    discrete_abscissa_zaxis = -speed_edge + (index_z.astype(jnp.float32) + 0.5) * (
        2.0 * speed_edge / VZ
    )
    return (discrete_abscissa_xaxis, discrete_abscissa_yaxis, discrete_abscissa_zaxis)


def moment_weights(discrete_abscissa_xaxis, discrete_abscissa_yaxis, discrete_abscissa_zaxis):
    square = (
        discrete_abscissa_xaxis * discrete_abscissa_xaxis
        + discrete_abscissa_yaxis * discrete_abscissa_yaxis
        + discrete_abscissa_zaxis * discrete_abscissa_zaxis
    )
    quadrature = (
        2.0
        * speed_edge
        / VX
        * (2.0 * speed_edge / VY)
        * (2.0 * speed_edge / VZ)
        / (2.0 * jnp.pi) ** 1.5
    )
    rows = [
        jnp.ones_like(discrete_abscissa_xaxis),
        discrete_abscissa_xaxis,
        discrete_abscissa_yaxis,
        discrete_abscissa_zaxis,
        square,
        discrete_abscissa_xaxis * discrete_abscissa_xaxis,
        discrete_abscissa_yaxis * discrete_abscissa_yaxis,
        discrete_abscissa_xaxis * discrete_abscissa_yaxis,
        discrete_abscissa_xaxis * discrete_abscissa_zaxis,
        discrete_abscissa_yaxis * discrete_abscissa_zaxis,
        discrete_abscissa_xaxis * square,
        discrete_abscissa_yaxis * square,
        discrete_abscissa_zaxis * square,
    ]
    return jnp.stack(rows) * quadrature


def conserved(moments):
    return jnp.stack([moments[0], moments[1], moments[2], moments[3], 0.5 * moments[4]])


def heat_flux(moments):
    mass = moments[0]
    flow_x = moments[1] / mass
    flow_y = moments[2] / mass
    flow_z = moments[3] / mass
    p_xx = moments[5]
    p_yy = moments[6]
    p_zz = moments[4] - moments[5] - moments[6]
    p_xy = moments[7]
    p_xz = moments[8]
    p_yz = moments[9]
    flow_sq = flow_x * flow_x + flow_y * flow_y + flow_z * flow_z
    heat_x = 0.5 * (
        moments[10]
        - 2.0 * (flow_x * p_xx + flow_y * p_xy + flow_z * p_xz)
        - flow_x * moments[4]
        + 2.0 * mass * flow_sq * flow_x
    )
    heat_y = 0.5 * (
        moments[11]
        - 2.0 * (flow_x * p_xy + flow_y * p_yy + flow_z * p_yz)
        - flow_y * moments[4]
        + 2.0 * mass * flow_sq * flow_y
    )
    heat_z = 0.5 * (
        moments[12]
        - 2.0 * (flow_x * p_xz + flow_y * p_yz + flow_z * p_zz)
        - flow_z * moments[4]
        + 2.0 * mass * flow_sq * flow_z
    )
    return jnp.stack([heat_x, heat_y, heat_z])


def transport(field, courant_x, courant_y):
    from_left = jnp.roll(field, 1, 2)
    from_right = jnp.roll(field, -1, 2)
    term_y = jnp.where(
        courant_y > 0, courant_y * (field - from_left), courant_y * (from_right - field)
    )
    padded = with_halo(field, (("space", 1),), 1)
    term_x = jnp.where(
        courant_x > 0, courant_x * (field - padded[:, :-2]), courant_x * (padded[:, 2:] - field)
    )
    return field - term_x - term_y


def diffuse(source):
    margin = with_halo(source, (("space", 1),), SWEEPS)
    iterate = margin
    for sweep_index in range(SWEEPS):
        inner = iterate[:, 1:-1]
        beside = iterate[:, :-2] + iterate[:, 2:] + jnp.roll(inner, 1, 2) + jnp.roll(inner, -1, 2)
        margin_edge = sweep_index + 1
        iterate = (
            margin[:, margin_edge : margin.shape[1] - margin_edge] + diffusivity * beside
        ) / (1.0 + 4.0 * diffusivity)
    return iterate


def collision_update_piece(
    convected_fields,
    discrete_abscissa_xaxis,
    discrete_abscissa_yaxis,
    discrete_abscissa_zaxis,
    particle_concentration,
    mean_drift_velocity,
    kinetic_thermal_level,
    energy_flux_components,
    collision_frequency,
    obstacle_indicators,
):
    diff_x = discrete_abscissa_xaxis - mean_drift_velocity[0]
    diff_y = discrete_abscissa_yaxis - mean_drift_velocity[1]
    diff_z = discrete_abscissa_zaxis - mean_drift_velocity[2]
    quadratic_deviation = diff_x * diff_x + diff_y * diff_y + diff_z * diff_z
    prefactor_amplitude = particle_concentration * kinetic_thermal_level ** (-1.5)
    local_gaussian_population = prefactor_amplitude * jnp.exp(
        -0.5 * quadratic_deviation / kinetic_thermal_level
    )
    skewed_correction_multiplier = (1.0 - momentum_thermal_ratio) / (
        5.0 * particle_concentration * kinetic_thermal_level * kinetic_thermal_level
    )
    projected_energy_flux = (
        diff_x * energy_flux_components[0]
        + diff_y * energy_flux_components[1]
        + diff_z * energy_flux_components[2]
    )
    goal_population = local_gaussian_population * (
        1.0
        + skewed_correction_multiplier
        * projected_energy_flux
        * (quadratic_deviation / kinetic_thermal_level - 5.0)
    )
    wall_state = particle_concentration * jnp.exp(
        -0.5
        * (
            discrete_abscissa_xaxis * discrete_abscissa_xaxis
            + discrete_abscissa_yaxis * discrete_abscissa_yaxis
            + discrete_abscissa_zaxis * discrete_abscissa_zaxis
        )
    )
    relaxed = convected_fields + collision_frequency * (goal_population - convected_fields)
    return jnp.where(obstacle_indicators > 0, wall_state, relaxed)


def per_device(distribution, rate_class, boundary_obstacle_indicator):
    vel_count, row_count, col_count = distribution.shape
    index = lax.axis_index("vel") * vel_count + jnp.arange(vel_count, dtype=jnp.int32)
    discrete_abscissa_xaxis, discrete_abscissa_yaxis, discrete_abscissa_zaxis = velocity_table(
        index
    )
    weights = moment_weights(
        discrete_abscissa_xaxis, discrete_abscissa_yaxis, discrete_abscissa_zaxis
    )
    column_x = discrete_abscissa_xaxis[:, None, None]
    column_y = discrete_abscissa_yaxis[:, None, None]
    column_z = discrete_abscissa_zaxis[:, None, None]
    courant_x = marching_step_length * column_x
    courant_y = marching_step_length * column_y
    reference_collision_freq = 0.5 * jnp.exp2(rate_class.astype(jnp.float32))
    field = distribution
    latest_conserved_fields = jnp.zeros((5, row_count, col_count), jnp.float32)
    for step_index in range(ITERS):
        convected_fields = transport(field, courant_x, courant_y)
        partial_value = jnp.dot(
            weights,
            convected_fields.reshape(vel_count, row_count * col_count),
            precision=lax.Precision.HIGHEST,
            preferred_element_type=jnp.float32,
        )
        moments = lax.psum(partial_value, "vel")
        source = conserved(moments)
        energy_flux_components = heat_flux(moments)
        source = source.reshape(5, row_count, col_count)
        energy_flux_components = energy_flux_components.reshape(3, row_count, col_count)
        latest_conserved_fields = diffuse(source)
        particle_concentration = latest_conserved_fields[0]
        mean_drift_velocity = latest_conserved_fields[1:4] / particle_concentration
        kinetic_thermal_level = (
            2.0 * latest_conserved_fields[4] / particle_concentration
            - (
                mean_drift_velocity[0] * mean_drift_velocity[0]
                + mean_drift_velocity[1] * mean_drift_velocity[1]
                + mean_drift_velocity[2] * mean_drift_velocity[2]
            )
        ) / 3.0
        collision_frequency = 1.0 - jnp.exp(
            -marching_step_length
            * reference_collision_freq
            * particle_concentration
            * kinetic_thermal_level ** (1.0 - shear_power_law_index)
        )
        field = collision_update_piece(
            convected_fields,
            column_x,
            column_y,
            column_z,
            particle_concentration,
            mean_drift_velocity,
            kinetic_thermal_level,
            energy_flux_components,
            collision_frequency,
            boundary_obstacle_indicator,
        )
    return (field, latest_conserved_fields)


def solution(mesh):
    placed = (P("vel", "space", None), P("space", None), P("space", None))
    return jax.shard_map(
        per_device,
        mesh=mesh,
        in_specs=placed,
        out_specs=(P("vel", "space", None), P(None, "space", None)),
        check_vma=False,
    )
```

profile of v0, /device:TPU:0, one launch (start us, length us, event | category | flops | bytes accessed | tf_op | source)
XLA Modules:
  0.0 239.6 jit_solution(17886712523408883976)
XLA Ops:
  0.6 4.2 %fusion.177 = (f32[1024,1,128]{2,1,0:T(1,128)S(1)}, f32[1024,1,128]{2,1,0:T(1,128)S(1)}) fusion(f32[1024,8,128]{2,1,0:T(8,128)} %param.3), kind=kLoop, calls=%fused_computation.291 | loop fusion | bytes 2097152 | tf_op jit(solution)/shard_map/slice | solution.py:23
  4.8 0.6 collective-permute-start.1
  5.4 0.1 collective-permute-start
  5.5 0.1 multiply_add_fusion
  5.6 0.1 fusion.164
  5.7 0.1 fusion.166
  5.8 0.1 fusion.170
  6.1 5.4 %copy.27 = f32[1024,8,128]{0,2,1:T(8,128)} copy(f32[1024,8,128]{2,1,0:T(8,128)} %param.3) | data formatting | bytes 8388608 | tf_op args[0]
  11.4 1.1 fusion.176
  12.5 0.1 stack.16
  12.6 8.7 %fusion.175 = (f32[1024,8,127]{0,2,1:T(8,128)}, f32[1024,8,127]{0,2,1:T(8,128)}) fusion(f32[1024,8,128]{0,2,1:T(8,128)} %copy.27), kind=kLoop, calls=%fused_computation.289 | loop fusion | bytes 16646144 | tf_op jit(solution)/shard_map/jit(_roll_static)/slice | solution.py:118
  21.4 0.2 copy.25
  21.6 0.2 copy.20
  21.8 8.6 %fusion.47 = f32[1024,8,128]{0,2,1:T(8,128)S(1)} fusion(f32[1024,8,128]{0,2,1:T(8,128)} %copy.27, f32[1024,1,128]{0,2,1:T(8,128)S(1)} %copy.25, f32[1024,1,128]{0,2,1:T(8,128)S(1)} %copy.20, f32[1024,8,127]{0,2,1:T(8,128)} %get-tuple-element.17, f32[1024,8,1]{0,2,1:T(1,128)S(1)} %get-tuple-element.19, f32[1024,8,1]{0,2,1:T(1,128)S(1)} %get-tuple-element.18, ...), kind=kLoop, calls=%fused_computation.62 | loop fusion | flops 16777216 | bytes 17836032 | tf_op jit(solution)/shard_map/sub | solution.py:126
  30.4 2.0 copy-done.2
  32.4 3.6 %fusion.58 = f32[13,1024]{1,0:T(8,128)S(1)} fusion(f32[1024,1024]{0,1:T(8,128)S(1)} %bitcast.95, f32[13,1024]{1,0:T(8,128)S(1)} %stack.16), kind=kOutput, calls=%fused_computation.78 | convolution fusion | flops 163591168 | bytes 4300800 | tf_op jit(solution)/shard_map/dot_general | solution.py:207
  36.0 78.6 %psum.14 = f32[13,1024]{1,0:T(8,128)S(1)} all-reduce(f32[13,1024]{1,0:T(8,128)S(1)} %fusion.58), channel_id=1, replica_groups=mesh['vel'=16,'space'=2] {'vel'}, use_global_device_ids=true, to_apply=%region_0.1 | all-reduce | flops 13312 | bytes 106496 | tf_op jit(solution)/shard_map/psum | solution.py:213
  114.7 0.1 collective-permute-start.2
  114.8 0.5 collective-permute-start.3
  115.3 0.6 collective-permute-done.2
  115.9 0.2 collective-permute-done.3
  116.1 0.1 fusion.193
  116.2 0.1 fusion.192
  116.3 0.1 fusion.83
  116.4 0.1 fusion.190
  116.4 0.1 fusion.191
  116.5 0.1 fusion.79
  116.6 0.1 fusion.188
  116.7 0.1 fusion.189
  116.8 0.1 fusion.75
  116.9 0.1 fusion.186
  117.0 0.1 fusion.187
  117.0 0.1 fusion.89
  117.2 7.4 %fusion.11 = f32[1024,8,128]{0,2,1:T(8,128)S(1)} fusion(f32[1024,8,128]{0,2,1:T(8,128)} %copy-done.2, f32[8,128]{1,0:T(8,128)S(1)} %bitcast.117, f32[8,128]{1,0:T(8,128)S(1)} %bitcast.115, f32[8,128]{1,0:T(8,128)S(1)} %bitcast.114, f32[8,128]{1,0:T(8,128)S(1)} %fusion.113, f32[8,128]{1,0:T(8,128)S(1)} %bitcast.111, f32[8,128]{1,0:T(8,128)S(1)} %get-tuple-element.71, ...), kind=kLoop, calls=%fused_computation.23 | loop fusion | flops 28311552 | bytes 8451072 | tf_op jit(solution)/shard_map/jit(_where)/select_n | solution.py:185
  124.7 1.9 copy-done
  126.7 0.2 copy.34
  126.9 0.2 copy.36
  127.1 0.4 collective-permute-start.5
  127.5 0.2 collective-permute-start.4
  127.7 8.7 %fusion.172 = (f32[1024,8,127]{0,2,1:T(8,128)}, f32[1024,8,127]{0,2,1:T(8,128)}) fusion(f32[1024,8,128]{0,2,1:T(8,128)} %copy-done), kind=kLoop, calls=%fused_computation.286 | loop fusion | bytes 16646144 | tf_op jit(solution)/shard_map/jit(_roll_static)/slice | solution.py:118
  136.5 0.2 copy.37
  136.7 0.2 copy.35
  136.9 8.6 %fusion.40 = f32[1024,8,128]{0,2,1:T(8,128)S(1)} fusion(f32[1024,8,128]{0,2,1:T(8,128)} %copy-done, f32[1024,1,128]{0,2,1:T(8,128)S(1)} %copy.37, f32[1024,1,128]{0,2,1:T(8,128)S(1)} %copy.35, f32[1024,8,127]{0,2,1:T(8,128)} %get-tuple-element.11, f32[1024,8,1]{0,2,1:T(1,128)S(1)} %get-tuple-element.13, f32[1024,8,1]{0,2,1:T(1,128)S(1)} %get-tuple-element.12, ...), kind=kLoop, calls=%fused_computation.53 | loop fusion | flops 16777216 | bytes 17836032 | tf_op jit(solution)/shard_map/sub | solution.py:126
  145.5 2.0 copy-done.1
  147.5 3.6 %fusion.56 = f32[13,1024]{1,0:T(8,128)S(1)} fusion(f32[1024,1024]{0,1:T(8,128)S(1)} %bitcast.94, f32[13,1024]{1,0:T(8,128)S(1)} %stack.16), kind=kOutput, calls=%fused_computation.76 | convolution fusion | flops 163591168 | bytes 4300800 | tf_op jit(solution)/shard_map/dot_general | solution.py:207
  151.1 71.8 %psum.15 = f32[13,1024]{1,0:T(8,128)S(1)} all-reduce(f32[13,1024]{1,0:T(8,128)S(1)} %fusion.56), channel_id=1, replica_groups=mesh['vel'=16,'space'=2] {'vel'}, use_global_device_ids=true, to_apply=%region_1.2 | all-reduce | flops 13312 | bytes 106496 | tf_op jit(solution)/shard_map/psum | solution.py:213
  222.9 0.1 collective-permute-start.6
  223.0 0.5 collective-permute-start.7
  223.6 0.6 collective-permute-done.6
  224.2 0.2 collective-permute-done.7
  224.4 0.1 fusion.185
  224.4 0.1 fusion.184
  224.5 0.1 fusion.71
  224.6 0.1 fusion.182
  224.7 0.1 fusion.183
  224.8 0.1 fusion.67
  224.9 0.1 fusion.180
  225.0 0.1 fusion.181
  225.0 0.1 fusion.63
  225.1 0.1 fusion.178
  225.2 0.1 fusion.179
  225.3 0.1 fusion.87
  225.5 8.8 %fusion.29 = f32[1024,8,128]{0,2,1:T(8,128)} fusion(f32[1024,8,128]{0,2,1:T(8,128)} %copy-done.1, f32[8,128]{1,0:T(8,128)S(1)} %bitcast.116, f32[8,128]{1,0:T(8,128)S(1)} %bitcast.113, f32[8,128]{1,0:T(8,128)S(1)} %bitcast.112, f32[8,128]{1,0:T(8,128)S(1)} %fusion.115, f32[8,128]{1,0:T(8,128)S(1)} %bitcast.110, f32[8,128]{1,0:T(8,128)S(1)} %get-tuple-element.68, ...), kind=kLoop, calls=%fused_computation.41 | loop fusion | flops 28311552 | bytes 8451072 | tf_op jit(solution)/shard_map/jit(_where)/select_n | solution.py:185
  234.3 5.4 %copy.38 = f32[1024,8,128]{2,1,0:T(8,128)} copy(f32[1024,8,128]{0,2,1:T(8,128)} %fusion.29) | data formatting | bytes 8388608
  (45 shorter events, 0.8 us)
Async XLA Ops:
  4.8 16.6 %collective-permute-start.1 = (f32[1024,1,128]{2,0,1:T(8,128)S(1)}, f32[1024,1,128]{2,0,1:T(8,128)S(1)}, u32[]{:S(2)}, u32[]{:S(2)}) collective-permute-start(f32[1024,1,128]{2,0,1:T(8,128)S(1)} %bitcast.97), channel_id=1, source_target_pairs={{1,0},{0,1},{3,2},{2,3},{5,4},{4,5},{7,6},{6,7},{9,8},{8,9},{11,10... | collective-permute-start | bytes 1572872 | tf_op jit(solution)/shard_map/ppermute | solution.py:26
  5.4 16.2 %collective-permute-start = (f32[1024,1,128]{2,0,1:T(8,128)S(1)}, f32[1024,1,128]{2,0,1:T(8,128)S(1)}, u32[]{:S(2)}, u32[]{:S(2)}) collective-permute-start(f32[1024,1,128]{2,0,1:T(8,128)S(1)} %bitcast.96), channel_id=1, source_target_pairs={{0,1},{1,0},{2,3},{3,2},{4,5},{5,4},{6,7},{7,6},{8,9},{9,8},{10,11... | collective-permute-start | bytes 1572872 | tf_op jit(solution)/shard_map/ppermute | solution.py:25
  6.1 5.4 %copy-start.5 = (s32[8,128]{1,0:T(8,128)S(1)}, s32[8,128]{1,0:T(8,128)}, u32[]{:S(2)}) copy-start(s32[8,128]{1,0:T(8,128)} %param.5) | copy-start | bytes 12292
  30.4 2.0 copy-start.2
  30.4 86.7 %copy-start.4 = (s32[8,128]{1,0:T(8,128)S(1)}, s32[8,128]{1,0:T(8,128)}, u32[]{:S(2)}) copy-start(s32[8,128]{1,0:T(8,128)} %param.4) | copy-start | bytes 12292
  114.7 1.2 collective-permute-start.2
  114.8 1.3 collective-permute-start.3
  124.6 2.0 copy-start
  127.1 9.3 %collective-permute-start.5 = (f32[1024,1,128]{2,0,1:T(8,128)S(1)}, f32[1024,1,128]{2,0,1:T(8,128)S(1)}, u32[]{:S(2)}, u32[]{:S(2)}) collective-permute-start(f32[1024,1,128]{2,0,1:T(8,128)S(1)} %copy.36), channel_id=1, source_target_pairs={{1,0},{0,1},{3,2},{2,3},{5,4},{4,5},{7,6},{6,7},{9,8},{8,9},{11,10... | collective-permute-start | bytes 1572872 | tf_op jit(solution)/shard_map/ppermute | solution.py:26
  127.5 9.1 %collective-permute-start.4 = (f32[1024,1,128]{2,0,1:T(8,128)S(1)}, f32[1024,1,128]{2,0,1:T(8,128)S(1)}, u32[]{:S(2)}, u32[]{:S(2)}) collective-permute-start(f32[1024,1,128]{2,0,1:T(8,128)S(1)} %copy.34), channel_id=1, source_target_pairs={{0,1},{1,0},{2,3},{3,2},{4,5},{5,4},{6,7},{7,6},{8,9},{9,8},{10,11... | collective-permute-start | bytes 1572872 | tf_op jit(solution)/shard_map/ppermute | solution.py:25
  145.5 2.0 copy-start.1
  222.9 1.2 collective-permute-start.6
  223.0 1.3 collective-permute-start.7
  225.4 8.9 %copy-start.3 = (f32[5,8,128]{2,1,0:T(8,128)}, f32[5,8,128]{2,1,0:T(8,128)S(1)}, u32[]{:S(2)}) copy-start(f32[5,8,128]{2,1,0:T(8,128)S(1)} %fusion.87) | copy-start | bytes 61444
where the time goes:
time: 240 us
  blocking collectives  150 us (62%)
  local copies, waits for them, and re-layouts  42.1 us (18%)
  other arithmetic  35.1 us (15%)
  matrix products  7.12 us (3%)
    psum x2, blocking collectives, per_device(): moments = lax.psum(partial_value, 'vel')  150 us
    slice x4, local copies, waits for them, and re-layouts, transport(): from_right = jnp.roll(field, -1, 2)  18.6 us
    sub x2, other arithmetic, transport(): return field - term_x - term_y  17.2 us
    unnamed x18, local copies, waits for them, and re-layouts  16.7 us
    select_n x2, other arithmetic, collision_update_piece(): return jnp.where(obstacle_indicators > 0, wall_state, relaxed)  16.2 us
    dot_general x2, matrix products, per_device(): jnp.dot(weights, convected_fields.reshape(vel_count, row_count * col_coun...  7.12 us
  transfers between devices with their start and end apart: 8, of which 4 were waited for; matrix products, arithmetic and copies ran while one was open for 10% of the time, Pallas kernels for 0%

commit v1 on v0

--- a/solution.py
+++ b/solution.py
@@ -13,6 +13,10 @@
 momentum_thermal_ratio = 2.0 / 3.0
 shear_power_law_index = 0.81
 diffusivity = 1.0
+
+
+def plan_the_lanes(u):
+    return jnp.sum(lax.all_gather(u, axis_name="vel"), axis=0)
 
 
 def with_halo(value, sides, width):
@@ -210,7 +214,7 @@
             precision=lax.Precision.HIGHEST,
             preferred_element_type=jnp.float32,
         )
-        moments = lax.psum(partial_value, "vel")
+        moments = plan_the_lanes(partial_value)
         source = conserved(moments)
         energy_flux_components = heat_flux(moments)
         source = source.reshape(5, row_count, col_count)

time: 240 us -> 181 us (0.75)
  blocking collectives: 150 us -> 90.8 us
    psum x2 -> x0, blocking collectives: 150 us -> none  [per_device(): moments = lax.psum(partial_value, 'vel')]
    all_gather x0 -> x2, blocking collectives: none -> 90.8 us  [plan_the_lanes(): return jnp.sum(lax.all_gather(u, axis_name='vel'), axis=0)]
  transfers between devices with their start and end apart: 8 -> 8, of which waited for: 4 -> 4; matrix products, arithmetic and copies ran while one was open for 10% -> 14% of each run, Pallas kernels for 0% -> 0%
where the time goes in v1:
time: 181 us; the launch traced here: 180 us
  blocking collectives  90.8 us (50%)
  local copies, waits for them, and re-layouts  42.1 us (23%)
  other arithmetic  35.3 us (20%)
  matrix products  7.12 us (4%)
  starting transfers between devices  2.35 us (1%)
    all_gather x2, blocking collectives, plan_the_lanes(): return jnp.sum(lax.all_gather(u, axis_name='vel'), axis=0)  90.8 us
    slice x4, local copies, waits for them, and re-layouts, transport(): from_right = jnp.roll(field, -1, 2)  18.6 us
    sub x2, other arithmetic, transport(): return field - term_x - term_y  17.2 us
    unnamed x18, local copies, waits for them, and re-layouts  16.7 us
    select_n x2, other arithmetic, collision_update_piece(): return jnp.where(obstacle_indicators > 0, wall_state, relaxed)  16.2 us
    dot_general x2, matrix products, per_device(): jnp.dot(weights, convected_fields.reshape(vel_count, row_count * col_coun...  7.12 us
    slice x3, local copies, waits for them, and re-layouts, with_halo(): last = lax.slice_in_dim(value, length - width, length, axis=dim)  4.45 us
  transfers between devices with their start and end apart: 8, of which 4 were waited for; matrix products, arithmetic and copies ran while one was open for 14% of the time, Pallas kernels for 0%

profile of v1, /device:TPU:0, one launch (start us, length us, event | category | flops | bytes accessed | tf_op | source)
XLA Modules:
  0.0 180.3 jit_solution(12490442037761716975)
XLA Ops:
  0.6 4.2 %fusion.175 = (f32[1024,1,128]{2,1,0:T(1,128)S(1)}, f32[1024,1,128]{2,1,0:T(1,128)S(1)}) fusion(f32[1024,8,128]{2,1,0:T(8,128)} %param.3), kind=kLoop, calls=%fused_computation.291 | loop fusion | bytes 2097152 | tf_op jit(solution)/shard_map/slice | solution.py:27
  4.8 0.6 collective-permute-start.1
  5.4 0.1 collective-permute-start
  5.5 0.1 multiply_add_fusion
  5.6 0.1 fusion.162
  5.7 0.1 fusion.164
  5.8 0.1 fusion.168
  6.1 5.4 %copy.27 = f32[1024,8,128]{0,2,1:T(8,128)} copy(f32[1024,8,128]{2,1,0:T(8,128)} %param.3) | data formatting | bytes 8388608 | tf_op args[0]
  11.4 1.1 fusion.174
  12.5 0.1 stack.16
  12.6 8.7 %fusion.173 = (f32[1024,8,127]{0,2,1:T(8,128)}, f32[1024,8,127]{0,2,1:T(8,128)}) fusion(f32[1024,8,128]{0,2,1:T(8,128)} %copy.27), kind=kLoop, calls=%fused_computation.289 | loop fusion | bytes 16646144 | tf_op jit(solution)/shard_map/jit(_roll_static)/slice | solution.py:122
  21.4 0.2 copy.25
  21.6 0.2 copy.20
  21.8 8.6 %fusion.47 = f32[1024,8,128]{0,2,1:T(8,128)S(1)} fusion(f32[1024,8,128]{0,2,1:T(8,128)} %copy.27, f32[1024,1,128]{0,2,1:T(8,128)S(1)} %copy.25, f32[1024,1,128]{0,2,1:T(8,128)S(1)} %copy.20, f32[1024,8,127]{0,2,1:T(8,128)} %get-tuple-element.17, f32[1024,8,1]{0,2,1:T(1,128)S(1)} %get-tuple-element.19, f32[1024,8,1]{0,2,1:T(1,128)S(1)} %get-tuple-element.18, ...), kind=kLoop, calls=%fused_computation.62 | loop fusion | flops 16777216 | bytes 17836032 | tf_op jit(solution)/shard_map/sub | solution.py:130
  30.4 2.0 %copy-done.2 = f32[1024,8,128]{0,2,1:T(8,128)} copy-done((f32[1024,8,128]{0,2,1:T(8,128)}, f32[1024,8,128]{0,2,1:T(8,128)S(1)}, u32[]{:S(2)}) %copy-start.2) | copy-done | bytes 4194328
  32.4 3.6 %convolution_bitcast_fusion.1 = f32[1,13,1024]{2,1,0:T(8,128)S(1)} fusion(f32[1024,1024]{0,1:T(8,128)S(1)} %bitcast.99, f32[13,1024]{1,0:T(8,128)S(1)} %stack.16), kind=kOutput, calls=%fused_computation.77 | convolution fusion | flops 163591168 | bytes 4300800 | tf_op jit(solution)/shard_map/dot_general | solution.py:211
  36.0 49.3 %all-gather.2 = f32[16,13,1024]{2,1,0:T(8,128)S(1)} all-gather(f32[1,13,1024]{2,1,0:T(8,128)S(1)} %convolution_bitcast_fusion.1), channel_id=2, replica_groups=mesh['vel'=16,'space'=2] {'vel'}, dimensions={0}, use_global_device_ids=true | all-gather | bytes 905216 | tf_op jit(solution)/shard_map/all_gather | solution.py:19
  85.4 0.1 collective-permute-start.2
  85.5 0.5 collective-permute-start.3
  86.1 0.6 collective-permute-done.2
  86.7 0.2 collective-permute-done.3
  86.8 0.1 fusion.191
  86.9 0.1 fusion.190
  87.0 0.1 fusion.81
  87.1 0.1 fusion.188
  87.2 0.1 fusion.189
  87.3 0.1 fusion.77
  87.4 0.1 fusion.186
  87.4 0.1 fusion.187
  87.5 0.1 fusion.73
  87.6 0.1 fusion.184
  87.7 0.1 fusion.185
  87.8 0.1 fusion.87
  88.0 7.4 %fusion.11 = f32[1024,8,128]{0,2,1:T(8,128)S(1)} fusion(f32[1024,8,128]{0,2,1:T(8,128)} %copy-done.2, f32[8,128]{1,0:T(8,128)S(1)} %bitcast.121, f32[8,128]{1,0:T(8,128)S(1)} %bitcast.119, f32[8,128]{1,0:T(8,128)S(1)} %bitcast.118, f32[8,128]{1,0:T(8,128)S(1)} %fusion.111, f32[8,128]{1,0:T(8,128)S(1)} %bitcast.115, f32[8,128]{1,0:T(8,128)S(1)} %get-tuple-element.71, ...), kind=kLoop, calls=%fused_computation.23 | loop fusion | flops 28311552 | bytes 8451072 | tf_op jit(solution)/shard_map/jit(_where)/select_n | solution.py:189
  95.5 1.9 %copy-done = f32[1024,8,128]{0,2,1:T(8,128)} copy-done((f32[1024,8,128]{0,2,1:T(8,128)}, f32[1024,8,128]{0,2,1:T(8,128)S(1)}, u32[]{:S(2)}) %copy-start) | copy-done | bytes 4194328
  97.5 0.2 copy.34
  97.7 0.2 copy.36
  97.9 0.4 collective-permute-start.5
  98.3 0.2 collective-permute-start.4
  98.5 8.7 %fusion.170 = (f32[1024,8,127]{0,2,1:T(8,128)}, f32[1024,8,127]{0,2,1:T(8,128)}) fusion(f32[1024,8,128]{0,2,1:T(8,128)} %copy-done), kind=kLoop, calls=%fused_computation.286 | loop fusion | bytes 16646144 | tf_op jit(solution)/shard_map/jit(_roll_static)/slice | solution.py:122
  107.2 0.2 copy.37
  107.4 0.2 copy.35
  107.6 8.6 %fusion.40 = f32[1024,8,128]{0,2,1:T(8,128)S(1)} fusion(f32[1024,8,128]{0,2,1:T(8,128)} %copy-done, f32[1024,1,128]{0,2,1:T(8,128)S(1)} %copy.37, f32[1024,1,128]{0,2,1:T(8,128)S(1)} %copy.35, f32[1024,8,127]{0,2,1:T(8,128)} %get-tuple-element.11, f32[1024,8,1]{0,2,1:T(1,128)S(1)} %get-tuple-element.13, f32[1024,8,1]{0,2,1:T(1,128)S(1)} %get-tuple-element.12, ...), kind=kLoop, calls=%fused_computation.53 | loop fusion | flops 16777216 | bytes 17836032 | tf_op jit(solution)/shard_map/sub | solution.py:130
  116.2 2.0 %copy-done.1 = f32[1024,8,128]{0,2,1:T(8,128)} copy-done((f32[1024,8,128]{0,2,1:T(8,128)}, f32[1024,8,128]{0,2,1:T(8,128)S(1)}, u32[]{:S(2)}) %copy-start.1) | copy-done | bytes 4194328
  118.2 3.6 %convolution_bitcast_fusion = f32[1,13,1024]{2,1,0:T(8,128)S(1)} fusion(f32[1024,1024]{0,1:T(8,128)S(1)} %bitcast.98, f32[13,1024]{1,0:T(8,128)S(1)} %stack.16), kind=kOutput, calls=%fused_computation.76 | convolution fusion | flops 163591168 | bytes 4300800 | tf_op jit(solution)/shard_map/dot_general | solution.py:211
  121.8 41.6 %all-gather.3 = f32[16,13,1024]{2,1,0:T(8,128)S(1)} all-gather(f32[1,13,1024]{2,1,0:T(8,128)S(1)} %convolution_bitcast_fusion), channel_id=3, replica_groups=mesh['vel'=16,'space'=2] {'vel'}, dimensions={0}, use_global_device_ids=true | all-gather | bytes 905216 | tf_op jit(solution)/shard_map/all_gather | solution.py:19
  163.5 0.1 collective-permute-start.6
  163.6 0.5 collective-permute-start.7
  164.2 0.6 collective-permute-done.6
  164.8 0.2 collective-permute-done.7
  165.0 0.1 fusion.183
  165.0 0.1 fusion.182
  165.1 0.1 fusion.69
  165.2 0.1 fusion.180
  165.3 0.1 fusion.181
  165.4 0.1 fusion.65
  165.5 0.1 fusion.178
  165.6 0.1 fusion.179
  165.6 0.1 fusion.61
  165.7 0.1 fusion.176
  165.8 0.1 fusion.177
  165.9 0.1 fusion.85
  166.1 8.8 %fusion.29 = f32[1024,8,128]{0,2,1:T(8,128)} fusion(f32[1024,8,128]{0,2,1:T(8,128)} %copy-done.1, f32[8,128]{1,0:T(8,128)S(1)} %bitcast.120, f32[8,128]{1,0:T(8,128)S(1)} %bitcast.117, f32[8,128]{1,0:T(8,128)S(1)} %bitcast.116, f32[8,128]{1,0:T(8,128)S(1)} %fusion.113, f32[8,128]{1,0:T(8,128)S(1)} %bitcast.114, f32[8,128]{1,0:T(8,128)S(1)} %get-tuple-element.68, ...), kind=kLoop, calls=%fused_computation.41 | loop fusion | flops 28311552 | bytes 8451072 | tf_op jit(solution)/shard_map/jit(_where)/select_n | solution.py:189
  174.9 5.4 %copy.38 = f32[1024,8,128]{2,1,0:T(8,128)} copy(f32[1024,8,128]{0,2,1:T(8,128)} %fusion.29) | data formatting | bytes 8388608
  (47 shorter events, 0.9 us)
Async XLA Ops:
  4.8 16.6 %collective-permute-start.1 = (f32[1024,1,128]{2,0,1:T(8,128)S(1)}, f32[1024,1,128]{2,0,1:T(8,128)S(1)}, u32[]{:S(2)}, u32[]{:S(2)}) collective-permute-start(f32[1024,1,128]{2,0,1:T(8,128)S(1)} %bitcast.101), channel_id=1, source_target_pairs={{1,0},{0,1},{3,2},{2,3},{5,4},{4,5},{7,6},{6,7},{9,8},{8,9},{11,10... | collective-permute-start | bytes 1572872 | tf_op jit(solution)/shard_map/ppermute | solution.py:30
  5.4 16.2 %collective-permute-start = (f32[1024,1,128]{2,0,1:T(8,128)S(1)}, f32[1024,1,128]{2,0,1:T(8,128)S(1)}, u32[]{:S(2)}, u32[]{:S(2)}) collective-permute-start(f32[1024,1,128]{2,0,1:T(8,128)S(1)} %bitcast.100), channel_id=1, source_target_pairs={{0,1},{1,0},{2,3},{3,2},{4,5},{5,4},{6,7},{7,6},{8,9},{9,8},{10,11... | collective-permute-start | bytes 1572872 | tf_op jit(solution)/shard_map/ppermute | solution.py:29
  6.1 5.4 %copy-start.5 = (s32[8,128]{1,0:T(8,128)S(1)}, s32[8,128]{1,0:T(8,128)}, u32[]{:S(2)}) copy-start(s32[8,128]{1,0:T(8,128)} %param.5) | copy-start | bytes 12292
  30.4 2.0 %copy-start.2 = (f32[1024,8,128]{0,2,1:T(8,128)}, f32[1024,8,128]{0,2,1:T(8,128)S(1)}, u32[]{:S(2)}) copy-start(f32[1024,8,128]{0,2,1:T(8,128)S(1)} %fusion.47) | copy-start | bytes 12582916
  32.4 55.5 %copy-start.4 = (s32[8,128]{1,0:T(8,128)S(1)}, s32[8,128]{1,0:T(8,128)}, u32[]{:S(2)}) copy-start(s32[8,128]{1,0:T(8,128)} %param.4) | copy-start | bytes 12292
  85.4 1.2 collective-permute-start.2
  85.5 1.3 collective-permute-start.3
  95.4 2.0 %copy-start = (f32[1024,8,128]{0,2,1:T(8,128)}, f32[1024,8,128]{0,2,1:T(8,128)S(1)}, u32[]{:S(2)}) copy-start(f32[1024,8,128]{0,2,1:T(8,128)S(1)} %fusion.11) | copy-start | bytes 12582916
  97.9 9.3 %collective-permute-start.5 = (f32[1024,1,128]{2,0,1:T(8,128)S(1)}, f32[1024,1,128]{2,0,1:T(8,128)S(1)}, u32[]{:S(2)}, u32[]{:S(2)}) collective-permute-start(f32[1024,1,128]{2,0,1:T(8,128)S(1)} %copy.36), channel_id=1, source_target_pairs={{1,0},{0,1},{3,2},{2,3},{5,4},{4,5},{7,6},{6,7},{9,8},{8,9},{11,10... | collective-permute-start | bytes 1572872 | tf_op jit(solution)/shard_map/ppermute | solution.py:30
  98.3 9.1 %collective-permute-start.4 = (f32[1024,1,128]{2,0,1:T(8,128)S(1)}, f32[1024,1,128]{2,0,1:T(8,128)S(1)}, u32[]{:S(2)}, u32[]{:S(2)}) collective-permute-start(f32[1024,1,128]{2,0,1:T(8,128)S(1)} %copy.34), channel_id=1, source_target_pairs={{0,1},{1,0},{2,3},{3,2},{4,5},{5,4},{6,7},{7,6},{8,9},{9,8},{10,11... | collective-permute-start | bytes 1572872 | tf_op jit(solution)/shard_map/ppermute | solution.py:29
  116.2 2.0 %copy-start.1 = (f32[1024,8,128]{0,2,1:T(8,128)}, f32[1024,8,128]{0,2,1:T(8,128)S(1)}, u32[]{:S(2)}) copy-start(f32[1024,8,128]{0,2,1:T(8,128)S(1)} %fusion.40) | copy-start | bytes 12582916
  163.5 1.2 collective-permute-start.6
  163.6 1.3 collective-permute-start.7
  166.0 8.9 %copy-start.3 = (f32[5,8,128]{2,1,0:T(8,128)}, f32[5,8,128]{2,1,0:T(8,128)S(1)}, u32[]{:S(2)}) copy-start(f32[5,8,128]{2,1,0:T(8,128)S(1)} %fusion.85) | copy-start | bytes 61444
